TPU v7x, 512 devices: a whole 4x8x8 slice. The times are simulated.
512 devices in a mesh: seq: 64 (over x, z, core), head: 8 (over y).
Axes of the slice: x: 4, y: 8, z: 8, core: 2. Of those that a mesh axis runs over, the one named last changes fastest.
Arguments:
- queries: bfloat16 [16384, 4096], P('seq', 'head'), may hold values from -6 to 6
- keys: bfloat16 [16384, 4096], P('seq', 'head'), may hold values from -6 to 6
- values: bfloat16 [16384, 4096], P('seq', 'head'), may hold values from -6 to 6
- gate: bfloat16 [16384, 4096], P('seq', 'head'), may hold values from -6 to 6
- residual: bfloat16 [16384, 4096], P('seq', 'head'), may hold values from -40 to 40
- log_decay: float32 [16384, 32], P('seq', 'head'), may hold values from -1 to 0, as said below
- out_weight: bfloat16 [4096, 4096], P('seq', 'head'), may hold values from -0.09375 to 0.09375
- norm_gain: bfloat16 [4096], P('head'), may hold values from 0.099609375 to 1.8984375
- kv_weight: bfloat16 [4096, 2048], P('seq', 'head'), may hold values from -0.09375 to 0.09375
Outputs:
- cache_keys: bfloat16 [16384, 1024], P('seq', 'head')
- cache_values: bfloat16 [16384, 1024], P('seq', 'head')
Inputs may be any that keep to these rules, and one draw needn't show every extreme that they name: `log_decay`: every entry is negative.
All inputs are finite; a program needn't handle non-finite values.
Results may differ from a plain program's by a relative error of at most 0.015.
Values may be sent and summed in bfloat16 or wider, within the bound.
A program may use at most 64 MiB of HBM per device.

v0:
```python
import jax
import jax.numpy as jnp
from jax import lax
from jax.sharding import PartitionSpec as P

HIGHEST = lax.Precision.HIGHEST


def entering(part, axis, combine, identity):
    place = lax.axis_index(axis)
    gathered = jax.tree.map(lambda a: lax.all_gather(a, axis), part)
    state = jax.tree.map(lambda a, e: jnp.zeros_like(a) + jnp.asarray(e, a.dtype), part, identity)

    def one(step, state):
        return combine(
            state, jax.tree.map(lambda a: lax.dynamic_index_in_dim(a, step, 0, False), gathered)
        )

    return lax.fori_loop(0, place, one, state)


def local_retention(queries, keys, values, log_decay, block):
    tokens, heads, width = queries.shape
    count = tokens // block

    def to_blocks(array):
        return array.reshape((count, block) + array.shape[1:])

    lower = jnp.arange(block)[:, None] >= jnp.arange(block)[None, :]

    def advance(carry, inputs):
        state, offset = carry
        query_block, key_block, value_block, decay_block = inputs
        within = jnp.cumsum(decay_block, axis=0)
        spread = within[:, None, :] - within[None, :, :]
        factor = jnp.where(
            lower[:, :, None], jnp.exp(jnp.where(lower[:, :, None], spread, 0.0)), 0.0
        )
        scores = jnp.einsum(
            "ihd,jhd->hij", query_block, key_block, preferred_element_type=jnp.float32
        )
        weighted = scores * jnp.transpose(factor, (2, 0, 1))
        values_wide = value_block.astype(jnp.float32)
        intra = jnp.einsum("hij,jhd->ihd", weighted, values_wide, precision=HIGHEST)
        query_wide = query_block.astype(jnp.float32)
        carried = jnp.exp(within)[:, :, None] * jnp.einsum(
            "ihd,hde->ihe", query_wide, state, precision=HIGHEST
        )
        ending = within[-1]
        key_wide = key_block.astype(jnp.float32) * jnp.exp(ending[None, :] - within)[:, :, None]
        fresh = jnp.exp(ending)[:, None, None] * state + jnp.einsum(
            "jhd,jhe->hde", key_wide, values_wide, precision=HIGHEST
        )
        return ((fresh, offset + ending), (intra + carried, offset[None, :] + within))

    start = (jnp.zeros((heads, width, width), jnp.float32), jnp.zeros((heads,), jnp.float32))
    final, stacked = lax.scan(
        advance,
        start,
        (to_blocks(queries), to_blocks(keys), to_blocks(values), to_blocks(log_decay)),
    )
    return (
        stacked[0].reshape(tokens, heads, width),
        stacked[1].reshape(tokens, heads),
        final[0],
        final[1],
    )


def combine_states(earlier, later):
    return (earlier[0] * later[0], later[0][:, None, None] * earlier[1] + later[1])


def on_device(queries, keys, values, gate, residual, log_decay, out_weight, norm_gain, kv_weight):
    tokens = queries.shape[0]
    heads = log_decay.shape[1]
    width = queries.shape[1] // heads
    shaped = [array.reshape(tokens, heads, width) for array in (queries, keys, values)]
    partial_out, running, state, offset = local_retention(
        shaped[0], shaped[1], shaped[2], log_decay, min(512, tokens)
    )
    identity = (jnp.ones((heads,), jnp.float32), jnp.zeros((heads, width, width), jnp.float32))
    scan_decay, incoming = entering((jnp.exp(offset), state), "seq", combine_states, identity)
    retained = partial_out + jnp.exp(running)[:, :, None] * jnp.einsum(
        "thd,hde->the", shaped[0].astype(jnp.float32), incoming, precision=HIGHEST
    )
    scale = lax.rsqrt(jnp.mean(retained * retained, axis=2, keepdims=True) + 1e-06)
    mixed = (
        jax.nn.silu(gate.astype(jnp.float32)) * (retained * scale).reshape(tokens, heads * width)
    ).astype(jnp.bfloat16)
    all_heads = lax.all_gather(mixed, "head", axis=1, tiled=True)
    out_full, kv_full = (
        lax.all_gather(out_weight, "seq", axis=0, tiled=True),
        lax.all_gather(kv_weight, "seq", axis=0, tiled=True),
    )
    branch = jnp.dot(all_heads, out_full, preferred_element_type=jnp.float32)
    hidden = (residual.astype(jnp.float32) + branch).astype(jnp.bfloat16)
    wide = hidden.astype(jnp.float32)
    squares = lax.psum(jnp.sum(wide * wide, axis=1), "head")
    features = wide.shape[1] * lax.axis_size("head")
    inverse = lax.rsqrt(squares[:, None] / features + 1e-06)
    local_norm = (wide * inverse * norm_gain.astype(jnp.float32)[None, :]).astype(jnp.bfloat16)
    normalized = lax.all_gather(local_norm, "head", axis=1, tiled=True)
    projected = jnp.dot(normalized, kv_full, preferred_element_type=jnp.float32)
    cache_heads = kv_weight.shape[1] // (2 * width)
    arranged = projected.reshape(tokens, cache_heads, 2, width)
    cache_keys = arranged[:, :, 0, :].reshape(tokens, cache_heads * width).astype(jnp.bfloat16)
    cache_values = arranged[:, :, 1, :].reshape(tokens, cache_heads * width).astype(jnp.bfloat16)
    return (cache_keys, cache_values)


def solution(mesh):
    placed = (
        P("seq", "head"),
        P("seq", "head"),
        P("seq", "head"),
        P("seq", "head"),
        P("seq", "head"),
        P("seq", "head"),
        P("seq", "head"),
        P("head"),
        P("seq", "head"),
    )
    return jax.shard_map(
        on_device,
        mesh=mesh,
        in_specs=placed,
        out_specs=(P("seq", "head"), P("seq", "head")),
        check_vma=False,
    )
```

profile of v0, /device:TPU:1, one launch (start us, length us, event | category | flops | bytes accessed | tf_op | source)
XLA Modules:
  0.0 388.1 jit_solution(8764286394529594663)
XLA Ops:
  7.2 0.0 copy-start
  7.2 0.0 all-gather.16.cloned.1.call-start
  7.2 0.7 reshape.72
  8.0 1.2 reduce-window.6
  9.2 0.1 slice.23
  9.2 0.1 copy.57
  9.4 0.1 copy.58
  9.5 0.1 add_bitcast_fusion
  9.6 0.2 slice_reduce_fusion
  9.8 0.1 bitcast_exponential_fusion
  9.8 1.1 copy.73
  10.9 2.0 convolution_add_fusion.1
  13.0 0.0 all-gather.16.cloned.1.call-update
  13.0 0.0 all-gather.10.cloned.1.call-start
  13.1 0.7 all-gather.10.cloned.1.call-update
  13.8 0.0 all-gather.8.cloned.1.call-start
  13.8 46.4 %all-gather.1 = f32[64,1,4]{2,1,0:T(1,128)S(1)} all-gather(f32[1,1,4]{2,1,0:T(1,128)S(1)} %bitcast.97), channel_id=1, replica_groups=mesh['seq'=64,'head'=8] {'seq'}, dimensions={0}, use_global_device_ids=true | all-gather | bytes 1040 | tf_op jit(solution)/shard_map/all_gather | solution.py:11
  60.2 0.0 copy-done
  60.2 0.4 fusion.2
  60.6 0.4 convolution_multiply_fusion
  61.0 64.0 %all-gather.16.cloned.1.call-done = f32[256,128,128]{2,1,0:T(8,128)} async-done(((f32[4,128,128]{2,1,0:T(8,128)}), f32[256,128,128]{2,1,0:T(8,128)}) %all-gather.16.cloned.1.call-update) | async-done | bytes 16777232 | tf_op jit(solution)/shard_map/all_gather | solution.py:11
  125.0 0.0 copy-start.1
  125.0 1.1 while.3
  125.1 1.1 bitcast_add_fusion.2
  126.2 0.4 fusion.3
  126.6 0.0 copy-done.1
  126.6 0.0 copy-start.2
  126.6 0.8 multiply_reduce_fusion.1
  127.4 0.0 copy-start.3
  127.4 0.0 copy-start.4
  127.5 0.2 copy.66
  127.7 0.0 copy-done.2
  127.7 0.9 fusion.12
  128.6 0.0 all-gather.8.cloned.1.call-update
  128.6 0.0 all-gather.14.cloned.1.call-start
  128.6 0.5 all-gather.14.cloned.1.call-update
  129.2 0.0 all-gather.12.cloned.1.call-start
  129.2 0.0 copy-done.3
  129.2 80.8 %all-gather.10.cloned.1.call-done = bf16[4096,512]{1,0:T(8,128)(2,1)} async-done(((bf16[64,512]{1,0:T(8,128)(2,1)}), bf16[4096,512]{1,0:T(8,128)(2,1)}) %all-gather.10.cloned.1.call-update) | async-done | bytes 4194320 | tf_op jit(solution)/shard_map/all_gather | solution.py:93
  210.1 38.3 %all-gather.8.cloned.1.call-done = bf16[256,4096]{1,0:T(8,128)(2,1)} async-done(((bf16[256,512]{1,0:T(8,128)(2,1)}), bf16[256,4096]{1,0:T(8,128)(2,1)}) %all-gather.8.cloned.1.call-update) | async-done | bytes 2097168 | tf_op jit(solution)/shard_map/all_gather | solution.py:91
  248.4 0.0 copy-done.4
  248.4 4.1 %multiply_reduce_fusion = (f32[256]{0:T(256)S(1)}, f32[256,512]{1,0:T(8,128)S(1)}) fusion(bf16[256,4096]{1,0:T(8,128)(2,1)} %all-gather.8.cloned.1.call-done, bf16[4096,512]{1,0:T(8,128)(2,1)} %all-gather.10.cloned.1.call-done, bf16[256,512]{1,0:T(8,128)(2,1)S(1)} %copy-done.4), kind=kOutput, calls=%fused_computation.22 | convolution fusion | flops 1074528000 | bytes 7078912 | tf_op jit(solution)/shard_map/dot_general | solution.py:96
  252.5 12.0 %psum.7 = f32[256]{0:T(256)S(1)} all-reduce(f32[256]{0:T(256)S(1)} %get-tuple-element.97), channel_id=1, replica_groups=mesh['seq'=64,'head'=8] {'head'}, use_global_device_ids=true, to_apply=%region_6.7 | all-reduce | flops 256 | bytes 2048 | tf_op jit(solution)/shard_map/psum | solution.py:99
  264.6 0.8 multiply_convert_fusion
  265.4 0.0 all-gather.12.cloned.1.call-update
  265.4 72.8 %all-gather.14.cloned.1.call-done = bf16[4096,256]{1,0:T(8,128)(2,1)} async-done(((bf16[64,256]{1,0:T(8,128)(2,1)}), bf16[4096,256]{1,0:T(8,128)(2,1)}) %all-gather.14.cloned.1.call-update) | async-done | bytes 2097168 | tf_op jit(solution)/shard_map/all_gather | solution.py:94
  338.2 38.7 %all-gather.12.cloned.1.call-done = bf16[256,4096]{1,0:T(8,128)(2,1)} async-done(((bf16[256,512]{1,0:T(8,128)(2,1)}), bf16[256,4096]{1,0:T(8,128)(2,1)}) %all-gather.12.cloned.1.call-update) | async-done | bytes 2097168 | tf_op jit(solution)/shard_map/all_gather | solution.py:103
  377.0 3.1 convolution_convert_fusion
  380.1 0.7 copy.71
  380.9 0.7 copy.72
  (12 shorter events, 0.2 us)
Async XLA Ops:
  7.2 53.0 %copy-start = (bf16[256,512]{1,0:T(8,128)(2,1)S(1)}, bf16[256,512]{1,0:T(8,128)(2,1)}, u32[]{:S(2)}) copy-start(bf16[256,512]{1,0:T(8,128)(2,1)} %param.11) | copy-start | bytes 786436
  7.2 117.8 %all-gather.16.cloned.1.call-start = ((), (), s32[]{:S(2)}) async-start(), calls=%async_computation.4 | async-start | bytes 17039360 | tf_op jit(solution)/shard_map/all_gather | solution.py:11
  13.0 197.1 %all-gather.10.cloned.1.call-start = ((), (), s32[]{:S(2)}) async-start(), calls=%async_computation.1 | async-start | bytes 4259840 | tf_op jit(solution)/shard_map/all_gather | solution.py:93
  13.8 234.6 %all-gather.8.cloned.1.call-start = ((), (), s32[]{:S(2)}) async-start(), calls=%async_computation | async-start | bytes 2359296 | tf_op jit(solution)/shard_map/all_gather | solution.py:91
  125.0 1.6 copy-start.1
  126.6 1.1 copy-start.2
  127.4 1.8 copy-start.3
  127.4 121.0 %copy-start.4 = (bf16[256,512]{1,0:T(8,128)(2,1)S(1)}, bf16[256,512]{1,0:T(8,128)(2,1)}, u32[]{:S(2)}) copy-start(bf16[256,512]{1,0:T(8,128)(2,1)} %param.15) | copy-start | bytes 786436
  128.6 209.6 %all-gather.14.cloned.1.call-start = ((), (), s32[]{:S(2)}) async-start(), calls=%async_computation.3 | async-start | bytes 2129920 | tf_op jit(solution)/shard_map/all_gather | solution.py:94
  129.2 247.8 %all-gather.12.cloned.1.call-start = ((), (), s32[]{:S(2)}) async-start(), calls=%async_computation.2 | async-start | bytes 2359296 | tf_op jit(solution)/shard_map/all_gather | solution.py:103
Sparse Core Ops, SparseCore 0:
  13.1 111.8 all-gather.15
  128.4 81.6 all-gather.9
  212.2 36.1 all-gather.7
  251.6 86.5 all-gather.13
  340.2 36.7 all-gather.11
where the time goes:
time: 393 us; the launch traced here: 388 us
  waiting for transfers between devices  296 us (75%)
  blocking collectives  58.4 us (15%)
  between operations  14 us (4%)
  matrix products  11.3 us (3%)
  other arithmetic  4.25 us (1%)
  local copies, waits for them, and re-layouts  4.04 us (1%)
    all_gather x1, waiting for transfers between devices, on_device(): lax.all_gather(out_weight, 'seq', axis=0, tiled=True)  80.8 us
    all_gather x1, waiting for transfers between devices, on_device(): lax.all_gather(kv_weight, 'seq', axis=0, tiled=True)  72.8 us
    all_gather x1, waiting for transfers between devices, entering(): gathered = jax.tree.map(lambda a: lax.all_gather(a, axis), part)  64 us
    all_gather x1, blocking collectives, entering(): gathered = jax.tree.map(lambda a: lax.all_gather(a, axis), part)  46.4 us
    all_gather x1, waiting for transfers between devices, on_device(): normalized = lax.all_gather(local_norm, 'head', axis=1, tiled=True)  38.7 us
    all_gather x1, waiting for transfers between devices, on_device(): all_heads = lax.all_gather(mixed, 'head', axis=1, tiled=True)  38.3 us
    psum x1, blocking collectives, on_device(): squares = lax.psum(jnp.sum(wide * wide, axis=1), 'head')  12 us
  transfers between devices with their start and end apart: 5, of which 5 were waited for; matrix products, arithmetic and copies ran while one was open for 2% of the time, Pallas kernels for 0%

commit v1 on v0

v1 whole, which is shorter than its diff:
```python
import functools

import jax
import jax.numpy as jnp
from jax import lax
from jax.experimental import pallas as pl
from jax.experimental.pallas import tpu as pltpu
from jax.sharding import PartitionSpec as P

MESH = pl.DeviceIdType.MESH
HIGHEST = lax.Precision.HIGHEST
F32, BF16 = jnp.float32, jnp.bfloat16

NX, NZ, NC, NY = 4, 8, 2, 8
GROUP = NZ * NC
TOK, WID, HEADS, HD = 256, 512, 4, 128
SLICE = HEADS * HD // GROUP
COPIES = 160
MIX_CHUNKS = 4
MIX_ROWS = TOK // MIX_CHUNKS
RED_CHUNKS = 2
RED_ROWS = TOK // RED_CHUNKS


def dot(a, b, dims=(((1,), (0,)), ((), ())), precision=None):
    return lax.dot_general(a, b, dims, precision=precision, preferred_element_type=F32)


NT = (((1,), (1,)), ((), ()))
TN = (((0,), (0,)), ((), ()))


def layer_kernel(
    q_h, k_h, v_h, g_h, r_h, ld_ref, ow_h, gain_ref, kw_h,
    ok_ref, ov_ref,
    q, k, v, g, res, wbuf, kvb, kin, wcol, st, rs, dec, xs, ex, ob, inc,
    intra, abuf, acc, hg, sr, sl, rr, rl, sq,
    lsem, ssem, rsem,
):
    seq, hy = lax.axis_index("seq"), lax.axis_index("head")
    sx, p = seq // GROUP, lax.rem(seq, GROUP)
    sz, sc = p // NC, lax.rem(p, NC)
    cc = 1 - sc

    def at(x, z, c, y):
        return (lax.rem(x + NX, NX) * GROUP + lax.rem(z + NZ, NZ) * NC + c, lax.rem(y + NY, NY))

    count = [0]
    unsent = []

    def remote(src, dst, device):
        i = count[0]
        count[0] += 1
        copy = pltpu.make_async_remote_copy(
            src_ref=src, dst_ref=dst, send_sem=ssem.at[i], recv_sem=rsem.at[i],
            device_id=device, device_id_type=MESH,
        )
        unsent.append(copy)
        return copy

    def send(src, dst, device):
        copy = remote(src, dst, device)
        copy.start()
        return copy

    def drain(keep=0):
        while len(unsent) > keep:
            unsent.pop(0).wait_send()

    loads = {}
    own_w = wbuf.at[sx, sz, sc]
    for i, (name, src, dst) in enumerate((
        ("k", k_h, k), ("v", v_h, v), ("w", ow_h, own_w), ("kw", kw_h, kin), ("q", q_h, q), ("g", g_h, g), ("r", r_h, res),
    )):
        loads[name] = pltpu.make_async_copy(src, dst, lsem.at[i])
        loads[name].start()

    swap_to = at(lax.rem(sz, NX), hy, cc, 2 * sx + sz // 4)
    swap_from = at(hy // 2, lax.rem(hy, 2) * 4 + sx, cc, sz)
    barrier = pltpu.get_barrier_semaphore()
    group_dev = [(sx * GROUP + lax.rem(p + i, GROUP), hy) for i in range(GROUP)]
    cross_dev = [at(sx + i, sz, sc, hy) for i in range(NX)]
    head_dev = [at(sx, sz, sc, hy + i) for i in range(NY)]
    greeted = group_dev[1:] + cross_dev[1:] + head_dev[1:] + [swap_to, swap_from]
    for device in greeted:
        pl.semaphore_signal(barrier, inc=1, device_id=device, device_id_type=MESH)

    rows = lax.broadcasted_iota(jnp.int32, (TOK, TOK), 0)
    cols = lax.broadcasted_iota(jnp.int32, (TOK, TOK), 1)
    lower = rows >= cols
    ld = jnp.concatenate([ld_ref[...], jnp.zeros((8 - HEADS, TOK), F32)], axis=0)
    wrow = dot(ld, (rows <= cols).astype(F32), precision=HIGHEST)
    within = dot(lower.astype(F32), ld, NT, precision=HIGHEST)
    wcol[...] = within
    dec[p] = jnp.broadcast_to(wrow[:, TOK - 1:TOK], (8, HD))

    pl.semaphore_wait(barrier, len(greeted))

    c_dec = [None] + [send(dec.at[p], dec.at[p], group_dev[i]) for i in range(1, GROUP)]
    loads["w"].wait()
    loads["kw"].wait()
    right_z, left_z = at(sx, sz + 1, sc, hy), at(sx, sz - 1, sc, hy)
    right_x, left_x = at(sx + 1, sz, sc, hy), at(sx - 1, sz, sc, hy)
    right_y, left_y = at(sx, sz, sc, hy + 1), at(sx, sz, sc, hy - 1)
    sibling = at(sx, sz, cc, hy)

    def wz(step, way):
        origin = lax.rem(sz - way * (step - 1) + NZ, NZ)
        if step < NZ // 2:
            part = wbuf.at[sx, origin, sc]
        else:
            part = wbuf.at[sx, origin, sc, pl.ds(0 if way == 1 else 32, 32)]
        return send(part, part, right_z if way == 1 else left_z)

    def wx(step, way):
        origin = lax.rem(sx - way * (step - 1) + NX, NX)
        if step == 1:
            part = wbuf.at[origin, :, sc]
        else:
            part = wbuf.at[origin, pl.ds(0 if way == 1 else NZ // 2, NZ // 2), sc]
        return send(part, part, right_x if way == 1 else left_x)

    def to_sibling(part):
        return send(part, part, sibling)

    def kz(step, way):
        origin = lax.rem(sz - way * (step - 1) + NZ, NZ)
        if step < NZ // 2:
            part = kvb.at[origin, :, cc]
        else:
            part = kvb.at[origin, pl.ds(0 if way == 1 else NX // 2, NX // 2), cc]
        return send(part, part, right_z if way == 1 else left_z)

    c_wz = {(1, way): wz(1, way) for way in (1, -1)}
    c_swap = send(kin, kvb.at[hy, lax.rem(sz, NX), sc], swap_to)

    def wz_step(step):
        for way in (1, -1):
            c_wz[step, way].wait_recv()
            if step < NZ // 2:
                c_wz[step + 1, way] = wz(step + 1, way)

    loads["k"].wait()
    loads["v"].wait()
    fade = jnp.exp(within[TOK - 1:TOK, :] - within)
    for h in range(HEADS):
        lanes = slice(h * HD, (h + 1) * HD)
        kd = (k[:, lanes].astype(F32) * fade[:, h:h + 1]).astype(BF16)
        st[lanes, :] = dot(kd, v[:, lanes], TN).astype(BF16)
    c_st = [None]
    for i in range(1, GROUP):
        there = lax.rem(p + i, GROUP)
        part = st.at[pl.ds(pl.multiple_of(there * SLICE, SLICE), SLICE)]
        c_st.append(send(part, rs.at[p], group_dev[i]))
    rs[p] = st[pl.ds(pl.multiple_of(p * SLICE, SLICE), SLICE), :]

    wz_step(1)

    loads["q"].wait()
    for h in range(HEADS):
        lanes = slice(h * HD, (h + 1) * HD)
        spread = within[:, h:h + 1] - wrow[h:h + 1, :]
        factor = jnp.exp(jnp.where(lower, spread, -1e30))
        scores = dot(q[:, lanes], k[:, lanes], NT)
        intra[:, lanes] = dot((scores * factor).astype(BF16), v[:, lanes])

    wz_step(2)
    c_swap.wait_recv()
    own_kv = kvb.at[sz, sx, cc]
    c_kx = [send(own_kv, own_kv, cross_dev[i]) for i in range(1, NX)]

    for i in range(1, GROUP):
        c_dec[i].wait_recv()
        c_st[i].wait_recv()
    row = pl.ds(p // (GROUP // HEADS), 1)
    state = jnp.zeros((SLICE, HD), F32)
    passed = jnp.zeros((1, HD), F32)
    before = []
    for i in range(GROUP):
        ex[i] = state
        before.append(passed)
        step = dec[i, row, :]
        state = jnp.exp(step) * state + rs[i].astype(F32)
        passed = passed + step
    xs[sx, 0:SLICE, :] = state
    xs[sx, SLICE:SLICE + 8, :] = jnp.broadcast_to(passed, (8, HD))
    c_xs = [send(xs.at[sx], xs.at[sx], cross_dev[i]) for i in range(1, NX)]

    wz_step(3)

    for copy in c_xs:
        copy.wait_recv()
    base = jnp.zeros((SLICE, HD), F32)
    for x in range(NX - 1):
        fresh = jnp.exp(xs[x, SLICE:SLICE + 1, :]) * base + xs[x, 0:SLICE, :]
        base = jnp.where(x < sx, fresh, base)
    for i in range(GROUP):
        ob[i] = (ex[i] + jnp.exp(before[i]) * base).astype(BF16)
    c_inc = []
    for i in range(1, GROUP):
        c_inc.append(send(ob.at[lax.rem(p + i, GROUP)], inc.at[p], group_dev[i]))
    inc[p] = ob[p]

    wz_step(4)
    c_wx = {(1, way): wx(1, way) for way in (1, -1)}
    c_sib = [to_sibling(wbuf.at[sx, :, sc])]
    for copy in c_kx:
        copy.wait_recv()

    loads["g"].wait()
    loads["r"].wait()
    for copy in c_inc:
        copy.wait_recv()

    c_kz = {(1, way): kz(1, way) for way in (1, -1)}
    c_sib.append(to_sibling(kvb.at[sz, :, cc]))

    def kz_step(step):
        for way in (1, -1):
            c_kz[step, way].wait_recv()
            origin = lax.rem(sz - way * step + NZ, NZ)
            if step < NZ // 2:
                c_kz[step + 1, way] = kz(step + 1, way)
                c_sib.append(to_sibling(kvb.at[origin, :, cc]))
            else:
                half = pl.ds(0 if way == 1 else NX // 2, NX // 2)
                c_sib.append(to_sibling(kvb.at[origin, half, cc]))

    def wx_step(step):
        for way in (1, -1):
            c_wx[step, way].wait_recv()
            origin = lax.rem(sx - way * step + NX, NX)
            if step == 1:
                c_wx[2, way] = wx(2, way)
                c_sib.append(to_sibling(wbuf.at[origin, :, sc]))
            else:
                half = pl.ds(0 if way == 1 else NZ // 2, NZ // 2)
                c_sib.append(to_sibling(wbuf.at[origin, half, sc]))

    c_mix = {}

    def mix_send(step, way, chunk):
        origin = lax.rem(hy - way * (step - 1) + NY, NY)
        part = abuf.at[origin, pl.ds(chunk * MIX_ROWS, MIX_ROWS)]
        c_mix[step, way, chunk] = send(part, part, right_y if way == 1 else left_y)

    def goes(step, way, chunk):
        if step < NY // 2:
            return True
        return (chunk < MIX_CHUNKS // 2) == (way == 1)

    grown = jnp.exp(within)
    for chunk in range(MIX_CHUNKS):
        span = slice(chunk * MIX_ROWS, (chunk + 1) * MIX_ROWS)
        for h in range(HEADS):
            lanes = slice(h * HD, (h + 1) * HD)
            entering = inc[4 * h:4 * h + 4].reshape(HD, HD)
            kept = intra[span, lanes] + grown[span, h:h + 1] * dot(q[span, lanes], entering)
            scale = lax.rsqrt(jnp.mean(kept * kept, axis=1, keepdims=True) + 1e-6)
            opened = g[span, lanes].astype(F32)
            opened = opened / (1.0 + jnp.exp(-opened))
            abuf[hy, span, lanes] = (opened * (kept * scale)).astype(BF16)
        for way in (1, -1):
            mix_send(1, way, chunk)

    for step in range(1, NY // 2):
        for chunk in range(MIX_CHUNKS):
            for way in (1, -1):
                c_mix[step, way, chunk].wait_recv()
                if goes(step + 1, way, chunk):
                    mix_send(step + 1, way, chunk)
        kz_step(step)
        if step < 3:
            wx_step(step)

    for copy in c_sib:
        copy.wait_recv()

    def project(origin):
        weight = wbuf[origin // 2, pl.ds(lax.rem(origin, 2) * 4, 4)].reshape(WID, WID)
        acc[...] += dot(abuf[origin], weight)

    acc[...] = res[...].astype(F32)

    def projected(i, carry):
        project(lax.rem(hy - (NY // 2 - 1) + i + NY, NY))
        return carry

    lax.fori_loop(0, NY - 1, projected, 0)
    for chunk in range(MIX_CHUNKS):
        for way in (1, -1):
            if goes(NY // 2, way, chunk):
                c_mix[NY // 2, way, chunk].wait_recv()
    project(lax.rem(hy + NY // 2, NY))

    hidden = acc[...].astype(BF16).astype(F32)
    squares = jnp.sum(hidden * hidden, axis=1, keepdims=True)
    sq[hy] = jnp.transpose(jnp.broadcast_to(squares, (TOK, HD)))[0:8, :]
    c_sq = [send(sq.at[hy], sq.at[hy], head_dev[i]) for i in range(1, NY)]
    hg[...] = (hidden * gain_ref[...].astype(F32)).astype(BF16)

    known = len(c_sib)
    kz_step(4)
    for copy in c_sib[known:]:
        copy.wait_recv()

    def partial(origin, span):
        return dot(hg[span, :], kvb[origin].reshape(WID, 2 * HD))

    c_red = {}
    half = NY // 2
    for step in range(half):
        for late in (False, True):
            for chunk in range(RED_CHUNKS):
                span = slice(chunk * RED_ROWS, (chunk + 1) * RED_ROWS)
                for way in (1, -1):
                    far = (chunk < RED_CHUNKS // 2) == (way == 1)
                    if step == 0 and not far:
                        continue
                    joins = step > 1 or (step == 1 and far)
                    if joins != late:
                        continue
                    out, came = (sr, rr) if way == 1 else (sl, rl)
                    value = partial(lax.rem(hy + way * (half - step) + NY, NY), span)
                    if joins:
                        c_red[step - 1, way, chunk].wait_recv()
                        value = value + came[step - 1, span, :].astype(F32)
                    out[step, span, :] = value.astype(BF16)
                    c_red[step, way, chunk] = send(
                        out.at[step, pl.ds(chunk * RED_ROWS, RED_ROWS)],
                        came.at[step, pl.ds(chunk * RED_ROWS, RED_ROWS)],
                        right_y if way == 1 else left_y,
                    )
    for copy in c_sq:
        copy.wait_recv()
    total = sq[0]
    for y in range(1, NY):
        total = total + sq[y]
    inverse = jnp.transpose(lax.rsqrt(total / (WID * NY) + 1e-6))
    for chunk in range(RED_CHUNKS):
        span = slice(chunk * RED_ROWS, (chunk + 1) * RED_ROWS)
        value = partial(hy, span)
        for way, came in ((1, rr), (-1, rl)):
            c_red[half - 1, way, chunk].wait_recv()
            value = value + came[half - 1, span, :].astype(F32)
        value = (value * inverse[span, 0:1]).astype(BF16)
        ok_ref[span, :] = value[:, :HD]
        ov_ref[span, :] = value[:, HD:]
    drain()


def on_device(queries, keys, values, gate, residual, log_decay, out_weight, norm_gain, kv_weight):
    anywhere = pl.BlockSpec(memory_space=pl.ANY)
    vmem = pl.BlockSpec(memory_space=pltpu.VMEM)
    block = pltpu.VMEM((TOK, WID), BF16)
    out = jax.ShapeDtypeStruct((TOK, HD), BF16)
    reds = pltpu.VMEM((NY // 2, TOK, 2 * HD), BF16)
    return pl.pallas_call(
        layer_kernel,
        out_shape=(out, out),
        in_specs=[anywhere] * 5 + [vmem, anywhere, vmem, anywhere],
        out_specs=(vmem, vmem),
        scratch_shapes=[
            block, block, block, block, block,
            pltpu.VMEM((NX, NZ, NC, 64, WID), BF16),
            pltpu.VMEM((NZ, NX, NC, 64, 2 * HD), BF16),
            pltpu.VMEM((64, 2 * HD), BF16),
            pltpu.VMEM((TOK, 8), F32),
            pltpu.VMEM((HEADS * HD, HD), BF16),
            pltpu.VMEM((GROUP, SLICE, HD), BF16),
            pltpu.VMEM((GROUP, 8, HD), F32),
            pltpu.VMEM((NX, SLICE + 8, HD), F32),
            pltpu.VMEM((GROUP, SLICE, HD), F32),
            pltpu.VMEM((GROUP, SLICE, HD), BF16),
            pltpu.VMEM((GROUP, SLICE, HD), BF16),
            pltpu.VMEM((TOK, WID), F32),
            pltpu.VMEM((NY, TOK, WID), BF16),
            pltpu.VMEM((TOK, WID), F32),
            block,
            reds, reds, reds, reds,
            pltpu.VMEM((NY, 8, TOK), F32),
            pltpu.SemaphoreType.DMA((8,)),
            pltpu.SemaphoreType.DMA((COPIES,)),
            pltpu.SemaphoreType.DMA((COPIES,)),
        ],
        compiler_params=pltpu.CompilerParams(
            collective_id=0, has_side_effects=True, vmem_limit_bytes=40 << 20
        ),
    )(
        queries, keys, values, gate, residual, log_decay.T, out_weight,
        norm_gain.reshape(1, WID), kv_weight,
    )


def solution(mesh):
    placed = (P("seq", "head"),) * 7 + (P("head"), P("seq", "head"))
    return jax.shard_map(
        on_device,
        mesh=mesh,
        in_specs=placed,
        out_specs=(P("seq", "head"), P("seq", "head")),
        check_vma=False,
    )
```

time: 393 us -> 95.5 us (0.24); the launches traced: 388 us -> 95.1 us
  waiting for transfers between devices: 296 us -> 0 us
  Pallas kernels: 0 us -> 86.2 us
  blocking collectives: 58.4 us -> 0 us
  between operations: 14 us -> 0.65 us
  matrix products: 11.3 us -> 0 us
  local copies, waits for them, and re-layouts: 4.04 us -> 8.3 us
  other arithmetic: 4.25 us -> 0 us
    all_gather x5 -> x0, waiting for transfers between devices: 295 us -> none  [the longest x1 80.8 us: on_device(): lax.all_gather(out_weight, 'seq', axis=0, tiled=True)]
    pallas_call x0 -> x1, Pallas kernels: none -> 86.2 us  [on_device(): pl.pallas_call(layer_kernel, out_shape=(out, out), in_specs=[anywhere] *...]
    all_gather x1 -> x0, blocking collectives: 46.4 us -> none  [entering(): gathered = jax.tree.map(lambda a: lax.all_gather(a, axis), part)]
    psum x1 -> x0, blocking collectives: 12 us -> none  [on_device(): squares = lax.psum(jnp.sum(wide * wide, axis=1), 'head')]
    dot_general x7 -> x0, matrix products: 11.3 us -> none  [the longest x1 4.15 us: on_device(): branch = jnp.dot(all_heads, out_full, preferred_element_type=jnp.float32)]
    unnamed x13 -> x18, local copies, waits for them, and re-layouts: 1.51 us -> 7.61 us
  transfers between devices with their start and end apart: 5 -> 0, of which waited for: 5 -> 0; matrix products, arithmetic and copies ran while one was open for 2% -> 0% of each run, Pallas kernels for 0% -> 0%
where the time goes in v1:
time: 95.5 us; the launch traced here: 95.1 us
  Pallas kernels  86.2 us (90%)
  local copies, waits for them, and re-layouts  8.3 us (9%)
    pallas_call x1, Pallas kernels, on_device(): pl.pallas_call(layer_kernel, out_shape=(out, out), in_specs=[anywhere] *...  86.2 us
    unnamed x18, local copies, waits for them, and re-layouts  7.61 us

profile of v1, /device:TPU:1, one launch (start us, length us, event | category | flops | bytes accessed | tf_op | source)
XLA Modules:
  0.0 95.1 jit_solution(15912558420651426792)
XLA Ops:
  0.6 0.0 copy-start.7
  0.6 0.7 reshape.7.gain_ref
  1.3 0.0 copy-done.7
  1.3 0.0 copy-start
  1.3 0.9 copy-done
  2.3 0.0 copy-start.1
  2.3 0.9 copy-done.1
  3.2 0.0 copy-start.2
  3.2 0.9 copy-done.2
  4.2 0.0 copy-start.3
  4.2 0.9 copy-done.3
  5.1 0.0 copy-start.4
  5.1 0.9 copy-done.4
  6.1 0.0 copy-start.5
  6.1 0.8 copy-done.5
  6.9 0.0 copy-start.6
  6.9 0.8 copy-done.6
  7.7 86.2 %shard_map.104 = (bf16[256,128]{1,0:T(8,128)(2,1)S(1)}, bf16[256,128]{1,0:T(8,128)(2,1)S(1)}) custom-call(bf16[256,512]{1,0:T(8,128)(2,1)S(1)} %copy-done, bf16[256,512]{1,0:T(8,128)(2,1)S(1)} %copy-done.1, bf16[256,512]{1,0:T(8,128)(2,1)S(1)} %copy-done.2, bf16[256,512]{1,0:T(8,128)(2,1)S(1)} %copy-done.3, bf16[256,512]{1,0:T(8,128)(2,1)S(1)} %copy-done.4, ...), custom_call_target="tpu_custom_call" | custom-call | tf_op jit(solution)/shard_map/pallas_call | solution.py:358
  93.8 0.6 copy.13
  94.5 0.6 copy.14
Async XLA Ops:
  0.6 0.7 copy-start.7
  1.3 1.0 copy-start
  2.3 0.9 copy-start.1
  3.2 0.9 copy-start.2
  4.2 0.9 copy-start.3
  5.1 0.9 copy-start.4
  6.1 0.8 copy-start.5
  6.9 0.8 copy-start.6

commit v2 on v1

v2 whole, which is shorter than its diff:
```python
import functools

import jax
import jax.numpy as jnp
from jax import lax
from jax.experimental import pallas as pl
from jax.experimental.pallas import tpu as pltpu
from jax.sharding import PartitionSpec as P

MESH = pl.DeviceIdType.MESH
HIGHEST = lax.Precision.HIGHEST
F32, BF16 = jnp.float32, jnp.bfloat16

NX, NZ, NC, NY = 4, 8, 2, 8
GROUP = NZ * NC
TOK, WID, HEADS, HD = 256, 512, 4, 128
SLICE = HEADS * HD // GROUP
CHUNKS = 4
ROWS = TOK // CHUNKS
COPIES = 105
ORDER = (0, 2, 1, 3)


def dot(a, b, dims=(((1,), (0,)), ((), ())), precision=None):
    return lax.dot_general(a, b, dims, precision=precision, preferred_element_type=F32)


NT = (((1,), (1,)), ((), ()))
TN = (((0,), (0,)), ((), ()))


def layer_kernel(
    q_h, k_h, v_h, g_h, r_h, ld_ref, ow_h, gain_ref, kw_h,
    out_ref,
    q, k, v, g, res, wbuf, kvb, kin, st, rs, dsr, dec, xs, ex, ob, inc,
    intra, abuf, acc, hg, red_out, red_in, scol, sq,
    lsem, sem,
):
    seq, hy = lax.axis_index("seq"), lax.axis_index("head")
    sx, p = seq // GROUP, lax.rem(seq, GROUP)
    sz, sc = p // NC, lax.rem(p, NC)
    cc = 1 - sc

    def at(x, z, c, y):
        return (lax.rem(x + NX, NX) * GROUP + lax.rem(z + NZ, NZ) * NC + c, lax.rem(y + NY, NY))

    count = [0]

    def new_sem():
        count[0] += 1
        return sem.at[count[0] - 1]

    home = at(sx, sz, cc, hy)
    drains = []

    class Stream:
        def __init__(self, whole):
            self.sent = new_sem()
            drains.append((whole, self.sent))

        def send(self, src, dst, device, came):
            copy = pltpu.make_async_remote_copy(
                src_ref=src, dst_ref=dst, send_sem=self.sent, recv_sem=came,
                device_id=device, device_id_type=MESH,
            )
            copy.start()
            return copy

    def arrived(whole, came):
        pltpu.make_async_remote_copy(
            src_ref=whole, dst_ref=whole, send_sem=came, recv_sem=came,
            device_id=home, device_id_type=MESH,
        ).wait_recv()

    loads = {}
    for i, (name, src, dst) in enumerate((
        ("w", ow_h, wbuf.at[sx, sz, sc]), ("kw", kw_h, kin), ("k", k_h, k), ("v", v_h, v),
        ("q", q_h, q), ("g", g_h, g), ("r", r_h, res),
    )):
        loads[name] = pltpu.make_async_copy(src, dst, lsem.at[i])
        loads[name].start()

    swap_to = at(lax.rem(sz, NX), hy, cc, 2 * sx + sz // 4)
    swap_from = at(hy // 2, lax.rem(hy, 2) * 4 + sx, cc, sz)
    barrier = pltpu.get_barrier_semaphore()
    group = [lax.rem(p + i, GROUP) for i in range(GROUP)]
    group_dev = [(sx * GROUP + there, hy) for there in group]
    cross_dev = [at(sx + i, sz, sc, hy) for i in range(NX)]
    head_dev = [at(sx, sz, sc, hy + i) for i in range(NY)]
    greeted = group_dev[1:] + cross_dev[1:] + head_dev[1:] + [swap_to, swap_from]
    for device in greeted:
        pl.semaphore_signal(barrier, inc=1, device_id=device, device_id_type=MESH)

    rows = lax.broadcasted_iota(jnp.int32, (TOK, TOK), 0)
    cols = lax.broadcasted_iota(jnp.int32, (TOK, TOK), 1)
    lower = rows >= cols
    ld = jnp.concatenate([ld_ref[...], jnp.zeros((8 - HEADS, TOK), F32)], axis=0)
    wrow = dot(ld, (rows <= cols).astype(F32), precision=HIGHEST)
    within = dot(lower.astype(F32), ld, NT, precision=HIGHEST)
    for h in range(HEADS):
        dsr[h] = jnp.broadcast_to(wrow[h:h + 1, TOK - 1:TOK], (1, HD))

    pl.semaphore_wait(barrier, len(greeted))

    right_z, left_z = at(sx, sz + 1, sc, hy), at(sx, sz - 1, sc, hy)
    right_x, left_x = at(sx + 1, sz, sc, hy), at(sx - 1, sz, sc, hy)
    right_y, left_y = at(sx, sz, sc, hy + 1), at(sx, sz, sc, hy - 1)

    s_wz = Stream(wbuf.at[0, pl.ds(0, NZ - 1), 0])
    s_wx = Stream(wbuf.at[pl.ds(0, NX - 1), :, 0])
    s_wc = Stream(wbuf.at[:, :, 0])
    s_kz = Stream(kvb.at[pl.ds(0, NZ - 1), :, 0])
    s_kc = Stream(kvb.at[:, :, 0])
    wc_came, kc_came = new_sem(), new_sem()
    wx_came = {1: new_sem(), -1: new_sem()}

    def wz(step, way):
        origin = lax.rem(sz - way * (step - 1) + NZ, NZ)
        if step < NZ // 2:
            part = wbuf.at[sx, origin, sc]
        else:
            part = wbuf.at[sx, origin, sc, pl.ds(0 if way == 1 else 32, 32)]
        return s_wz.send(part, part, right_z if way == 1 else left_z, new_sem())

    def wx_first(origin):
        part = wbuf.at[sx, origin, sc]
        for way in (1, -1):
            s_wx.send(part, part, right_x if way == 1 else left_x, wx_came[way])

    def wx_second(way):
        part = wbuf.at[lax.rem(sx - way + NX, NX), pl.ds(0 if way == 1 else NZ // 2, NZ // 2), sc]
        return s_wx.send(part, part, right_x if way == 1 else left_x, new_sem())

    def kz(step, way, half):
        origin = lax.rem(sz - way * (step - 1) + NZ, NZ)
        part = kvb.at[origin, pl.ds(half * 2, 2), cc]
        return s_kz.send(part, part, right_z if way == 1 else left_z, new_sem())

    def w_sibling(part):
        s_wc.send(part, part, home, wc_came)

    def k_sibling(part):
        s_kc.send(part, part, home, kc_came)

    s_dec, dec_came = Stream(dec.at[pl.ds(0, GROUP - 1)]), new_sem()
    for i in range(1, GROUP):
        s_dec.send(dsr.at[group[i] // (GROUP // HEADS)], dec.at[p], group_dev[i], dec_came)
    dec[p] = dsr[p // (GROUP // HEADS)]
    loads["w"].wait()
    c_wz = {(1, way): wz(1, way) for way in (1, -1)}
    wx_first(sz)
    loads["kw"].wait()
    c_swap = Stream(kin).send(kin, kvb.at[hy, lax.rem(sz, NX), sc], swap_to, new_sem())

    def wz_step(step):
        for way in (1, -1):
            c_wz[step, way].wait_recv()
            if step < NZ // 2:
                c_wz[step + 1, way] = wz(step + 1, way)
        for way in (1, -1):
            if step < NZ // 2 or way == 1:
                wx_first(lax.rem(sz - way * step + NZ, NZ))

    loads["k"].wait()
    loads["v"].wait()
    fade = jnp.exp(within[TOK - 1:TOK, :] - within)
    for h in range(HEADS):
        lanes = slice(h * HD, (h + 1) * HD)
        kd = (k[:, lanes].astype(F32) * fade[:, h:h + 1]).astype(BF16)
        st[h * 4:h * 4 + 4] = dot(kd, v[:, lanes], TN).astype(BF16).reshape(4, SLICE, HD)
    s_st, st_came = Stream(rs.at[pl.ds(0, GROUP - 1)]), new_sem()
    for i in range(1, GROUP):
        s_st.send(st.at[group[i]], rs.at[p], group_dev[i], st_came)
    rs[p] = st[p]

    wz_step(1)

    loads["q"].wait()
    for h in range(HEADS):
        lanes = slice(h * HD, (h + 1) * HD)
        spread = within[:, h:h + 1] - wrow[h:h + 1, :]
        factor = jnp.exp(jnp.where(lower, spread, -1e30))
        scores = dot(q[:, lanes], k[:, lanes], NT)
        intra[:, lanes] = dot((scores * factor).astype(BF16), v[:, lanes])

    wz_step(2)
    c_swap.wait_recv()
    own_kv = kvb.at[sz, sx, cc]
    s_kx, kx_came = Stream(kvb.at[0, pl.ds(0, NX - 1), 0]), new_sem()
    for i in range(1, NX):
        s_kx.send(own_kv, own_kv, cross_dev[i], kx_came)

    arrived(dec.at[pl.ds(0, GROUP - 1)], dec_came)
    arrived(rs.at[pl.ds(0, GROUP - 1)], st_came)
    state = jnp.zeros((SLICE, HD), F32)
    passed = jnp.zeros((1, HD), F32)
    before = []
    for i in range(GROUP):
        ex[i] = state
        before.append(passed)
        step = dec[i]
        state = jnp.exp(step) * state + rs[i].astype(F32)
        passed = passed + step
    xs[sx, 0:SLICE, :] = state
    xs[sx, SLICE:SLICE + 8, :] = jnp.broadcast_to(passed, (8, HD))
    s_xs, xs_came = Stream(xs.at[pl.ds(0, NX - 1)]), new_sem()
    for i in range(1, NX):
        s_xs.send(xs.at[sx], xs.at[sx], cross_dev[i], xs_came)

    wz_step(3)

    arrived(xs.at[pl.ds(0, NX - 1)], xs_came)
    base = jnp.zeros((SLICE, HD), F32)
    for x in range(NX - 1):
        fresh = jnp.exp(xs[x, SLICE:SLICE + 1, :]) * base + xs[x, 0:SLICE, :]
        base = jnp.where(x < sx, fresh, base)
    for i in range(GROUP):
        ob[i] = (ex[i] + jnp.exp(before[i]) * base).astype(BF16)
    s_inc, inc_came = Stream(ob.at[pl.ds(0, GROUP - 1)]), new_sem()
    for i in range(1, GROUP):
        s_inc.send(ob.at[group[i]], inc.at[p], group_dev[i], inc_came)
    inc[p] = ob[p]

    wz_step(4)
    w_sibling(wbuf.at[sx, :, sc])
    loads["g"].wait()
    loads["r"].wait()
    arrived(kvb.at[0, pl.ds(0, NX - 1), 0], kx_came)
    arrived(inc.at[pl.ds(0, GROUP - 1)], inc_came)

    c_kz = {(1, way, half): kz(1, way, half) for half in (0, 1) for way in (1, -1)}
    k_sibling(kvb.at[sz, :, cc])
    c_wx = {}

    def kz_step(step, half):
        for way in (1, -1):
            if (step, way, half) not in c_kz:
                continue
            c_kz[step, way, half].wait_recv()
            if step + 1 < NZ // 2 or (step + 1 == NZ // 2 and half == (0 if way == 1 else 1)):
                c_kz[step + 1, way, half] = kz(step + 1, way, half)
            origin = lax.rem(sz - way * step + NZ, NZ)
            k_sibling(kvb.at[origin, pl.ds(half * 2, 2), cc])

    def wx_step(step):
        for way in (1, -1):
            origin = lax.rem(sx - way * step + NX, NX)
            if step == 1:
                arrived(wbuf.at[0, :, 0], wx_came[way])
                c_wx[way] = wx_second(way)
                w_sibling(wbuf.at[origin, :, sc])
            else:
                c_wx[way].wait_recv()
                half = pl.ds(0 if way == 1 else NZ // 2, NZ // 2)
                w_sibling(wbuf.at[origin, half, sc])

    s_mix, c_mix = Stream(abuf.at[pl.ds(0, NY - 1)]), {}

    def far(chunk):
        return 1 if chunk < CHUNKS // 2 else -1

    def mix_send(step, way, chunk):
        if step == NY // 2 and way != far(chunk):
            return
        origin = lax.rem(hy - way * (step - 1) + NY, NY)
        part = abuf.at[origin, pl.ds(chunk * ROWS, ROWS)]
        c_mix[step, way, chunk] = s_mix.send(part, part, right_y if way == 1 else left_y, new_sem())

    grown = jnp.exp(within)
    for chunk in ORDER:
        span = slice(chunk * ROWS, (chunk + 1) * ROWS)
        for h in range(HEADS):
            lanes = slice(h * HD, (h + 1) * HD)
            entering = inc[4 * h:4 * h + 4].reshape(HD, HD)
            kept = intra[span, lanes] + grown[span, h:h + 1] * dot(q[span, lanes], entering)
            scale = lax.rsqrt(jnp.mean(kept * kept, axis=1, keepdims=True) + 1e-6)
            opened = g[span, lanes].astype(F32)
            opened = opened / (1.0 + jnp.exp(-opened))
            abuf[hy, span, lanes] = (opened * (kept * scale)).astype(BF16)
        for way in (1, -1):
            mix_send(1, way, chunk)

    service = {
        0: (lambda: wx_step(1),),
        1: (lambda: kz_step(1, 0),), 2: (lambda: kz_step(1, 1),),
        4: (lambda: kz_step(2, 0),), 5: (lambda: kz_step(2, 1),),
        6: (lambda: wx_step(2),),
        7: (lambda: kz_step(3, 0),), 8: (lambda: kz_step(3, 1),),
        10: (lambda: kz_step(4, 0), lambda: kz_step(4, 1)),
    }
    for step in range(1, NY // 2):
        for n, chunk in enumerate(ORDER):
            for way in (1, -1):
                c_mix[step, way, chunk].wait_recv()
                mix_send(step + 1, way, chunk)
            for job in service.get((step - 1) * CHUNKS + n, ()):
                job()

    arrived(wbuf.at[:, :, 0], wc_came)

    def weight(origin):
        return wbuf[origin // 2, pl.ds(lax.rem(origin, 2) * 4, 4)].reshape(WID, WID)

    acc[...] = res[...].astype(F32)

    def projected(i, carry):
        origin = lax.rem(hy - (NY // 2 - 1) + i + NY, NY)
        acc[...] += dot(abuf[origin], weight(origin))
        return carry

    lax.fori_loop(0, NY - 1, projected, 0)
    arrived(kvb.at[:, :, 0], kc_came)

    last = lax.rem(hy + NY // 2, NY)
    s_red, c_red = Stream(red_out.at[pl.ds(0, NY - 1)]), {}

    def reduce_send(step, way, chunk):
        span = slice(chunk * ROWS, (chunk + 1) * ROWS)
        slot = step * 2 + (0 if way == 1 else 1)
        origin = lax.rem(hy + way * (NY // 2 - step) + NY, NY)
        value = dot(hg[span, :], kvb[origin].reshape(WID, 2 * HD))
        if (step - 1, way, chunk) in c_red:
            c_red[step - 1, way, chunk].wait_recv()
            value = value + red_in[slot - 2, span, :].astype(F32)
        red_out[slot, span, :] = value.astype(BF16)
        c_red[step, way, chunk] = s_red.send(
            red_out.at[slot, pl.ds(chunk * ROWS, ROWS)], red_in.at[slot, pl.ds(chunk * ROWS, ROWS)],
            right_y if way == 1 else left_y, new_sem(),
        )

    gain = gain_ref[...].astype(F32).reshape(1, WID)
    for chunk in ORDER:
        span = slice(chunk * ROWS, (chunk + 1) * ROWS)
        c_mix[NY // 2, far(chunk), chunk].wait_recv()
        hidden = (acc[span, :] + dot(abuf[last, span, :], weight(last))).astype(BF16).astype(F32)
        hg[span, :] = (hidden * gain).astype(BF16)
        scol[span, :] = jnp.broadcast_to(jnp.sum(hidden * hidden, axis=1, keepdims=True), (ROWS, HD))
        reduce_send(0, far(chunk), chunk)
        reduce_send(1, -far(chunk), chunk)
    sq[hy] = jnp.transpose(scol[...])[0:8, :]
    s_sq, sq_came = Stream(sq.at[pl.ds(0, NY - 1)]), new_sem()
    for i in range(1, NY):
        s_sq.send(sq.at[hy], sq.at[hy], head_dev[i], sq_came)
    for chunk in ORDER:
        reduce_send(1, far(chunk), chunk)
    for step in range(2, NY // 2):
        for late in (False, True):
            for chunk in ORDER:
                reduce_send(step, far(chunk) if late else -far(chunk), chunk)
    arrived(sq.at[pl.ds(0, NY - 1)], sq_came)
    total = sq[0]
    for y in range(1, NY):
        total = total + sq[y]
    inverse = jnp.transpose(lax.rsqrt(total / (WID * NY) + 1e-6))
    for chunk in ORDER:
        span = slice(chunk * ROWS, (chunk + 1) * ROWS)
        value = dot(hg[span, :], kvb[hy].reshape(WID, 2 * HD))
        for way in (1, -1):
            c_red[NY // 2 - 1, way, chunk].wait_recv()
            slot = NY - 2 + (0 if way == 1 else 1)
            value = value + red_in[slot, span, :].astype(F32)
        out_ref[span, :] = (value * inverse[span, 0:1]).astype(BF16)

    assert count[0] <= COPIES, count[0]
    for whole, sent in drains:
        pltpu.make_async_remote_copy(
            src_ref=whole, dst_ref=whole, send_sem=sent, recv_sem=sent,
            device_id=home, device_id_type=MESH,
        ).wait_send()


def on_device(queries, keys, values, gate, residual, log_decay, out_weight, norm_gain, kv_weight):
    hbm = pl.BlockSpec(memory_space=pltpu.HBM)
    vmem = pl.BlockSpec(memory_space=pltpu.VMEM)
    block = pltpu.VMEM((TOK, WID), BF16)
    reds = pltpu.VMEM((NY, TOK, 2 * HD), BF16)
    slices = pltpu.VMEM((GROUP, SLICE, HD), BF16)
    both = pl.pallas_call(
        layer_kernel,
        out_shape=jax.ShapeDtypeStruct((TOK, 2 * HD), BF16),
        in_specs=[hbm] * 5 + [vmem, hbm, vmem, hbm],
        out_specs=vmem,
        scratch_shapes=[
            block, block, block, block, block,
            pltpu.VMEM((NX, NZ, NC, 64, WID), BF16),
            pltpu.VMEM((NZ, NX, NC, 64, 2 * HD), BF16),
            pltpu.VMEM((64, 2 * HD), BF16),
            slices,
            slices,
            pltpu.VMEM((HEADS, 1, HD), F32),
            pltpu.VMEM((GROUP, 1, HD), F32),
            pltpu.VMEM((NX, SLICE + 8, HD), F32),
            pltpu.VMEM((GROUP, SLICE, HD), F32),
            slices,
            slices,
            pltpu.VMEM((TOK, WID), F32),
            pltpu.VMEM((NY, TOK, WID), BF16),
            pltpu.VMEM((TOK, WID), F32),
            block,
            reds, reds,
            pltpu.VMEM((TOK, HD), F32),
            pltpu.VMEM((NY, 8, TOK), F32),
            pltpu.SemaphoreType.DMA((7,)),
            pltpu.SemaphoreType.DMA((COPIES,)),
        ],
        compiler_params=pltpu.CompilerParams(
            collective_id=0, has_side_effects=True, vmem_limit_bytes=62 << 20
        ),
    )(
        queries, keys, values, gate, residual, log_decay.T, out_weight, norm_gain, kv_weight,
    )
    return both[:, :HD], both[:, HD:]


def solution(mesh):
    placed = (P("seq", "head"),) * 7 + (P("head"), P("seq", "head"))
    return jax.shard_map(
        on_device,
        mesh=mesh,
        in_specs=placed,
        out_specs=(P("seq", "head"), P("seq", "head")),
        check_vma=False,
    )
```

time: 95.5 us -> 86.4 us (0.905)
  the two profiles are of different devices: /device:TPU:1 before, /device:TPU:8 now
where the time goes in v2:
time: 86.4 us; the launch traced here: 86.2 us
  Pallas kernels  84.1 us (97%)
  local copies, waits for them, and re-layouts  1.53 us (2%)
    pallas_call x1, Pallas kernels, on_device(): pl.pallas_call(layer_kernel, out_shape=jax.ShapeDtypeStruct((TOK, 2 * HD)...  84.1 us

profile of v2, /device:TPU:8, one launch (start us, length us, event | category | flops | bytes accessed | tf_op | source)
XLA Modules:
  0.0 86.2 jit_solution(1570782051343460582)
XLA Ops:
  0.6 84.1 %shard_map.104 = bf16[256,256]{1,0:T(8,128)(2,1)} custom-call(bf16[256,512]{1,0:T(8,128)(2,1)} %q_h.1, bf16[256,512]{1,0:T(8,128)(2,1)} %k_h.1, bf16[256,512]{1,0:T(8,128)(2,1)} %v_h.1, bf16[256,512]{1,0:T(8,128)(2,1)} %g_h.1, bf16[256,512]{1,0:T(8,128)(2,1)} %r_h.1, f32[4,256]{1,0:T(4,128)} %bitcast.1, bf16[64,512]{1,0:T(8,128)(2,1)} %ow_h.1, ...), custom_call_target="tpu_custom_call" | custom-call | tf_op jit(solution)/shard_map/pallas_call | solution.py:378
  84.7 1.5 %fusion = (bf16[256,128]{1,0:T(8,128)(2,1)}, bf16[256,128]{1,0:T(8,128)(2,1)}) fusion(bf16[256,256]{1,0:T(8,128)(2,1)} %shard_map.104), kind=kLoop, calls=%fused_computation | loop fusion | bytes 262144 | tf_op jit(solution)/shard_map/slice | solution.py:412

commit v3 on v2

--- a/solution.py
+++ b/solution.py
@@ -100,6 +100,14 @@
     for h in range(HEADS):
         dsr[h] = jnp.broadcast_to(wrow[h:h + 1, TOK - 1:TOK], (1, HD))
 
+    loads["k"].wait()
+    loads["v"].wait()
+    fade = jnp.exp(within[TOK - 1:TOK, :] - within)
+    for h in range(HEADS):
+        lanes = slice(h * HD, (h + 1) * HD)
+        kd = (k[:, lanes].astype(F32) * fade[:, h:h + 1]).astype(BF16)
+        st[h * 4:h * 4 + 4] = dot(kd, v[:, lanes], TN).astype(BF16).reshape(4, SLICE, HD)
+
     pl.semaphore_wait(barrier, len(greeted))
 
     right_z, left_z = at(sx, sz + 1, sc, hy), at(sx, sz - 1, sc, hy)
@@ -146,35 +154,21 @@
     for i in range(1, GROUP):
         s_dec.send(dsr.at[group[i] // (GROUP // HEADS)], dec.at[p], group_dev[i], dec_came)
     dec[p] = dsr[p // (GROUP // HEADS)]
-    loads["w"].wait()
-    c_wz = {(1, way): wz(1, way) for way in (1, -1)}
-    wx_first(sz)
-    loads["kw"].wait()
-    c_swap = Stream(kin).send(kin, kvb.at[hy, lax.rem(sz, NX), sc], swap_to, new_sem())
-
-    def wz_step(step):
-        for way in (1, -1):
-            c_wz[step, way].wait_recv()
-            if step < NZ // 2:
-                c_wz[step + 1, way] = wz(step + 1, way)
-        for way in (1, -1):
-            if step < NZ // 2 or way == 1:
-                wx_first(lax.rem(sz - way * step + NZ, NZ))
-
-    loads["k"].wait()
-    loads["v"].wait()
-    fade = jnp.exp(within[TOK - 1:TOK, :] - within)
-    for h in range(HEADS):
-        lanes = slice(h * HD, (h + 1) * HD)
-        kd = (k[:, lanes].astype(F32) * fade[:, h:h + 1]).astype(BF16)
-        st[h * 4:h * 4 + 4] = dot(kd, v[:, lanes], TN).astype(BF16).reshape(4, SLICE, HD)
     s_st, st_came = Stream(rs.at[pl.ds(0, GROUP - 1)]), new_sem()
     for i in range(1, GROUP):
         s_st.send(st.at[group[i]], rs.at[p], group_dev[i], st_came)
     rs[p] = st[p]
 
-    wz_step(1)
-
+    loads["w"].wait()
+    c_wz = {(1, way): wz(1, way) for way in (1, -1)}
+    loads["kw"].wait()
+    c_swap = Stream(kin).send(kin, kvb.at[hy, lax.rem(sz, NX), sc], swap_to, new_sem())
+
+    def wz_step(step):
+        for way in (1, -1):
+            c_wz[step, way].wait_recv()
+            if step < NZ // 2:
+                c_wz[step + 1, way] = wz(step + 1, way)
     loads["q"].wait()
     for h in range(HEADS):
         lanes = slice(h * HD, (h + 1) * HD)
@@ -183,12 +177,7 @@
         scores = dot(q[:, lanes], k[:, lanes], NT)
         intra[:, lanes] = dot((scores * factor).astype(BF16), v[:, lanes])
 
-    wz_step(2)
-    c_swap.wait_recv()
-    own_kv = kvb.at[sz, sx, cc]
-    s_kx, kx_came = Stream(kvb.at[0, pl.ds(0, NX - 1), 0]), new_sem()
-    for i in range(1, NX):
-        s_kx.send(own_kv, own_kv, cross_dev[i], kx_came)
+    wz_step(1)
 
     arrived(dec.at[pl.ds(0, GROUP - 1)], dec_came)
     arrived(rs.at[pl.ds(0, GROUP - 1)], st_came)
@@ -207,7 +196,7 @@
     for i in range(1, NX):
         s_xs.send(xs.at[sx], xs.at[sx], cross_dev[i], xs_came)
 
-    wz_step(3)
+    wz_step(2)
 
     arrived(xs.at[pl.ds(0, NX - 1)], xs_came)
     base = jnp.zeros((SLICE, HD), F32)
@@ -221,7 +210,18 @@
         s_inc.send(ob.at[group[i]], inc.at[p], group_dev[i], inc_came)
     inc[p] = ob[p]
 
+    c_swap.wait_recv()
+    own_kv = kvb.at[sz, sx, cc]
+    s_kx, kx_came = Stream(kvb.at[0, pl.ds(0, NX - 1), 0]), new_sem()
+    for i in range(1, NX):
+        s_kx.send(own_kv, own_kv, cross_dev[i], kx_came)
+    for step in (0, -1, 1, -2, 2):
+        wx_first(lax.rem(sz + step + NZ, NZ))
+    wz_step(3)
+    for step in (-3, 3):
+        wx_first(lax.rem(sz + step + NZ, NZ))
     wz_step(4)
+    wx_first(lax.rem(sz + NZ // 2, NZ))
     w_sibling(wbuf.at[sx, :, sc])
     loads["g"].wait()
     loads["r"].wait()
@@ -281,12 +281,12 @@
             mix_send(1, way, chunk)
 
     service = {
-        0: (lambda: wx_step(1),),
-        1: (lambda: kz_step(1, 0),), 2: (lambda: kz_step(1, 1),),
-        4: (lambda: kz_step(2, 0),), 5: (lambda: kz_step(2, 1),),
-        6: (lambda: wx_step(2),),
-        7: (lambda: kz_step(3, 0),), 8: (lambda: kz_step(3, 1),),
-        10: (lambda: kz_step(4, 0), lambda: kz_step(4, 1)),
+        0: (lambda: kz_step(1, 0),), 1: (lambda: kz_step(1, 1),),
+        2: (lambda: wx_step(1),),
+        3: (lambda: kz_step(2, 0),), 4: (lambda: kz_step(2, 1),),
+        6: (lambda: kz_step(3, 0),), 7: (lambda: kz_step(3, 1),),
+        8: (lambda: wx_step(2),),
+        9: (lambda: kz_step(4, 0), lambda: kz_step(4, 1)),
     }
     for step in range(1, NY // 2):
         for n, chunk in enumerate(ORDER):

time: 86.4 us -> 80.6 us (0.933)
  the two profiles are of different devices: /device:TPU:8 before, /device:TPU:2 now
where the time goes in v3:
time: 80.6 us; the launch traced here: 80.3 us
  Pallas kernels  78.2 us (97%)
  local copies, waits for them, and re-layouts  1.53 us (2%)
    pallas_call x1, Pallas kernels, on_device(): pl.pallas_call(layer_kernel, out_shape=jax.ShapeDtypeStruct((TOK, 2 * HD)...  78.2 us

profile of v3, /device:TPU:2, one launch (start us, length us, event | category | flops | bytes accessed | tf_op | source)
XLA Modules:
  0.0 80.3 jit_solution(16938174046889182364)
XLA Ops:
  0.6 78.2 %shard_map.104 = bf16[256,256]{1,0:T(8,128)(2,1)} custom-call(bf16[256,512]{1,0:T(8,128)(2,1)} %q_h.1, bf16[256,512]{1,0:T(8,128)(2,1)} %k_h.1, bf16[256,512]{1,0:T(8,128)(2,1)} %v_h.1, bf16[256,512]{1,0:T(8,128)(2,1)} %g_h.1, bf16[256,512]{1,0:T(8,128)(2,1)} %r_h.1, f32[4,256]{1,0:T(4,128)} %bitcast.1, bf16[64,512]{1,0:T(8,128)(2,1)} %ow_h.1, ...), custom_call_target="tpu_custom_call" | custom-call | tf_op jit(solution)/shard_map/pallas_call | solution.py:378
  78.8 1.5 %fusion = (bf16[256,128]{1,0:T(8,128)(2,1)}, bf16[256,128]{1,0:T(8,128)(2,1)}) fusion(bf16[256,256]{1,0:T(8,128)(2,1)} %shard_map.104), kind=kLoop, calls=%fused_computation | loop fusion | bytes 262144 | tf_op jit(solution)/shard_map/slice | solution.py:412

commit v4 on v3

--- a/solution.py
+++ b/solution.py
@@ -80,8 +80,14 @@
         loads[name] = pltpu.make_async_copy(src, dst, lsem.at[i])
         loads[name].start()
 
-    swap_to = at(lax.rem(sz, NX), hy, cc, 2 * sx + sz // 4)
-    swap_from = at(hy // 2, lax.rem(hy, 2) * 4 + sx, cc, sz)
+    swap_x, swap_z = lax.rem(hy, NX), jnp.where(hy < NX, sz, NZ - 1 - sz)
+    swap_to = at(swap_x, swap_z, cc, 2 * sx + sz // 4)
+
+    def kslot(z):
+        return jnp.where((z // 4) != lax.rem(hy, 2), NZ - 1 - lax.rem(z, 4), lax.rem(z, 4))
+
+    moved = (sz // 4) != lax.rem(hy, 2)
+    swap_from = at(hy // 2, jnp.where(moved, NZ - 1 - sz, sz), cc, sx + jnp.where(moved, NX, 0))
     barrier = pltpu.get_barrier_semaphore()
     group = [lax.rem(p + i, GROUP) for i in range(GROUP)]
     group_dev = [(sx * GROUP + there, hy) for there in group]
@@ -141,7 +147,7 @@
 
     def kz(step, way, half):
         origin = lax.rem(sz - way * (step - 1) + NZ, NZ)
-        part = kvb.at[origin, pl.ds(half * 2, 2), cc]
+        part = kvb.at[kslot(origin), pl.ds(half * 2, 2), cc]
         return s_kz.send(part, part, right_z if way == 1 else left_z, new_sem())
 
     def w_sibling(part):
@@ -161,8 +167,6 @@
 
     loads["w"].wait()
     c_wz = {(1, way): wz(1, way) for way in (1, -1)}
-    loads["kw"].wait()
-    c_swap = Stream(kin).send(kin, kvb.at[hy, lax.rem(sz, NX), sc], swap_to, new_sem())
 
     def wz_step(step):
         for way in (1, -1):
@@ -177,7 +181,11 @@
         scores = dot(q[:, lanes], k[:, lanes], NT)
         intra[:, lanes] = dot((scores * factor).astype(BF16), v[:, lanes])
 
-    wz_step(1)
+    loads["kw"].wait()
+    c_swap = Stream(kin).send(kin, kvb.at[4 * (hy // 4) + lax.rem(sz, 4), swap_x, sc], swap_to, new_sem())
+    loads["g"].wait()
+    opened = g[...].astype(F32)
+    acc[...] = opened / (1.0 + jnp.exp(-opened))
 
     arrived(dec.at[pl.ds(0, GROUP - 1)], dec_came)
     arrived(rs.at[pl.ds(0, GROUP - 1)], st_came)
@@ -196,7 +204,7 @@
     for i in range(1, NX):
         s_xs.send(xs.at[sx], xs.at[sx], cross_dev[i], xs_came)
 
-    wz_step(2)
+    wz_step(1)
 
     arrived(xs.at[pl.ds(0, NX - 1)], xs_came)
     base = jnp.zeros((SLICE, HD), F32)
@@ -211,25 +219,23 @@
     inc[p] = ob[p]
 
     c_swap.wait_recv()
-    own_kv = kvb.at[sz, sx, cc]
+    own_kv = kvb.at[kslot(sz), sx, cc]
     s_kx, kx_came = Stream(kvb.at[0, pl.ds(0, NX - 1), 0]), new_sem()
     for i in range(1, NX):
         s_kx.send(own_kv, own_kv, cross_dev[i], kx_came)
-    for step in (0, -1, 1, -2, 2):
+    for step in (0, -1, 1):
+        wx_first(lax.rem(sz + step + NZ, NZ))
+    wz_step(2)
+    for step in (-2, 2):
         wx_first(lax.rem(sz + step + NZ, NZ))
     wz_step(3)
     for step in (-3, 3):
         wx_first(lax.rem(sz + step + NZ, NZ))
-    wz_step(4)
-    wx_first(lax.rem(sz + NZ // 2, NZ))
-    w_sibling(wbuf.at[sx, :, sc])
-    loads["g"].wait()
     loads["r"].wait()
     arrived(kvb.at[0, pl.ds(0, NX - 1), 0], kx_came)
     arrived(inc.at[pl.ds(0, GROUP - 1)], inc_came)
 
-    c_kz = {(1, way, half): kz(1, way, half) for half in (0, 1) for way in (1, -1)}
-    k_sibling(kvb.at[sz, :, cc])
+    c_kz = {}
     c_wx = {}
 
     def kz_step(step, half):
@@ -240,7 +246,7 @@
             if step + 1 < NZ // 2 or (step + 1 == NZ // 2 and half == (0 if way == 1 else 1)):
                 c_kz[step + 1, way, half] = kz(step + 1, way, half)
             origin = lax.rem(sz - way * step + NZ, NZ)
-            k_sibling(kvb.at[origin, pl.ds(half * 2, 2), cc])
+            k_sibling(kvb.at[kslot(origin), pl.ds(half * 2, 2), cc])
 
     def wx_step(step):
         for way in (1, -1):
@@ -274,19 +280,22 @@
             entering = inc[4 * h:4 * h + 4].reshape(HD, HD)
             kept = intra[span, lanes] + grown[span, h:h + 1] * dot(q[span, lanes], entering)
             scale = lax.rsqrt(jnp.mean(kept * kept, axis=1, keepdims=True) + 1e-6)
-            opened = g[span, lanes].astype(F32)
-            opened = opened / (1.0 + jnp.exp(-opened))
-            abuf[hy, span, lanes] = (opened * (kept * scale)).astype(BF16)
+            abuf[hy, span, lanes] = (acc[span, lanes] * (kept * scale)).astype(BF16)
         for way in (1, -1):
             mix_send(1, way, chunk)
-
+        if chunk < 2:
+            for way in (1, -1):
+                c_kz[1, way, chunk] = kz(1, way, chunk)
+
+    wz_step(4)
+    wx_first(lax.rem(sz + NZ // 2, NZ))
+    w_sibling(wbuf.at[sx, :, sc])
+    k_sibling(kvb.at[kslot(sz), :, cc])
     service = {
         0: (lambda: kz_step(1, 0),), 1: (lambda: kz_step(1, 1),),
-        2: (lambda: wx_step(1),),
-        3: (lambda: kz_step(2, 0),), 4: (lambda: kz_step(2, 1),),
+        3: (lambda: kz_step(2, 0), lambda: wx_step(1)), 4: (lambda: kz_step(2, 1),),
         6: (lambda: kz_step(3, 0),), 7: (lambda: kz_step(3, 1),),
-        8: (lambda: wx_step(2),),
-        9: (lambda: kz_step(4, 0), lambda: kz_step(4, 1)),
+        9: (lambda: kz_step(4, 0), lambda: kz_step(4, 1), lambda: wx_step(2)),
     }
     for step in range(1, NY // 2):
         for n, chunk in enumerate(ORDER):
@@ -314,11 +323,14 @@
     last = lax.rem(hy + NY // 2, NY)
     s_red, c_red = Stream(red_out.at[pl.ds(0, NY - 1)]), {}
 
+    def cache_weight(origin):
+        return kvb[pl.ds(4 * (origin // 4), 4), lax.rem(origin, NX)].reshape(WID, 2 * HD)
+
     def reduce_send(step, way, chunk):
         span = slice(chunk * ROWS, (chunk + 1) * ROWS)
         slot = step * 2 + (0 if way == 1 else 1)
         origin = lax.rem(hy + way * (NY // 2 - step) + NY, NY)
-        value = dot(hg[span, :], kvb[origin].reshape(WID, 2 * HD))
+        value = dot(hg[span, :], cache_weight(origin))
         if (step - 1, way, chunk) in c_red:
             c_red[step - 1, way, chunk].wait_recv()
             value = value + red_in[slot - 2, span, :].astype(F32)
@@ -354,7 +366,7 @@
     inverse = jnp.transpose(lax.rsqrt(total / (WID * NY) + 1e-6))
     for chunk in ORDER:
         span = slice(chunk * ROWS, (chunk + 1) * ROWS)
-        value = dot(hg[span, :], kvb[hy].reshape(WID, 2 * HD))
+        value = dot(hg[span, :], cache_weight(hy))
         for way in (1, -1):
             c_red[NY // 2 - 1, way, chunk].wait_recv()
             slot = NY - 2 + (0 if way == 1 else 1)

time: 80.6 us -> 78.2 us (0.970)
  the two profiles are of different devices: /device:TPU:2 before, /device:TPU:1 now
where the time goes in v4:
time: 78.2 us; the launch traced here: 76.6 us
  Pallas kernels  74.4 us (95%)
  local copies, waits for them, and re-layouts  1.53 us (2%)
    pallas_call x1, Pallas kernels, on_device(): pl.pallas_call(layer_kernel, out_shape=jax.ShapeDtypeStruct((TOK, 2 * HD)...  74.4 us

profile of v4, /device:TPU:1, one launch (start us, length us, event | category | flops | bytes accessed | tf_op | source)
XLA Modules:
  0.0 76.6 jit_solution(456353149658104329)
XLA Ops:
  0.6 74.4 %shard_map.104 = bf16[256,256]{1,0:T(8,128)(2,1)} custom-call(bf16[256,512]{1,0:T(8,128)(2,1)} %q_h.1, bf16[256,512]{1,0:T(8,128)(2,1)} %k_h.1, bf16[256,512]{1,0:T(8,128)(2,1)} %v_h.1, bf16[256,512]{1,0:T(8,128)(2,1)} %g_h.1, bf16[256,512]{1,0:T(8,128)(2,1)} %r_h.1, f32[4,256]{1,0:T(4,128)} %bitcast.1, bf16[64,512]{1,0:T(8,128)(2,1)} %ow_h.1, ...), custom_call_target="tpu_custom_call" | custom-call | tf_op jit(solution)/shard_map/pallas_call | solution.py:390
  75.1 1.5 %fusion = (bf16[256,128]{1,0:T(8,128)(2,1)}, bf16[256,128]{1,0:T(8,128)(2,1)}) fusion(bf16[256,256]{1,0:T(8,128)(2,1)} %shard_map.104), kind=kLoop, calls=%fused_computation | loop fusion | bytes 262144 | tf_op jit(solution)/shard_map/slice | solution.py:424

commit v5 on v4

--- a/solution.py
+++ b/solution.py
@@ -25,6 +25,10 @@
     return lax.dot_general(a, b, dims, precision=precision, preferred_element_type=F32)
 
 
+def farthest(size):
+    return sorted(range(1, size), key=lambda i: (-min(i, size - i), i))
+
+
 NT = (((1,), (1,)), ((), ()))
 TN = (((0,), (0,)), ((), ()))
 
@@ -33,7 +37,7 @@
     q_h, k_h, v_h, g_h, r_h, ld_ref, ow_h, gain_ref, kw_h,
     out_ref,
     q, k, v, g, res, wbuf, kvb, kin, st, rs, dsr, dec, xs, ex, ob, inc,
-    intra, abuf, acc, hg, red_out, red_in, scol, sq,
+    intra, abuf, acc, hg, red_out, red_in, part, scol, sq,
     lsem, sem,
 ):
     seq, hy = lax.axis_index("seq"), lax.axis_index("head")
@@ -157,11 +161,11 @@
         s_kc.send(part, part, home, kc_came)
 
     s_dec, dec_came = Stream(dec.at[pl.ds(0, GROUP - 1)]), new_sem()
-    for i in range(1, GROUP):
+    for i in farthest(GROUP):
         s_dec.send(dsr.at[group[i] // (GROUP // HEADS)], dec.at[p], group_dev[i], dec_came)
     dec[p] = dsr[p // (GROUP // HEADS)]
     s_st, st_came = Stream(rs.at[pl.ds(0, GROUP - 1)]), new_sem()
-    for i in range(1, GROUP):
+    for i in farthest(GROUP):
         s_st.send(st.at[group[i]], rs.at[p], group_dev[i], st_came)
     rs[p] = st[p]
 
@@ -201,7 +205,7 @@
     xs[sx, 0:SLICE, :] = state
     xs[sx, SLICE:SLICE + 8, :] = jnp.broadcast_to(passed, (8, HD))
     s_xs, xs_came = Stream(xs.at[pl.ds(0, NX - 1)]), new_sem()
-    for i in range(1, NX):
+    for i in farthest(NX):
         s_xs.send(xs.at[sx], xs.at[sx], cross_dev[i], xs_came)
 
     wz_step(1)
@@ -214,14 +218,14 @@
     for i in range(GROUP):
         ob[i] = (ex[i] + jnp.exp(before[i]) * base).astype(BF16)
     s_inc, inc_came = Stream(ob.at[pl.ds(0, GROUP - 1)]), new_sem()
-    for i in range(1, GROUP):
+    for i in farthest(GROUP):
         s_inc.send(ob.at[group[i]], inc.at[p], group_dev[i], inc_came)
     inc[p] = ob[p]
 
     c_swap.wait_recv()
     own_kv = kvb.at[kslot(sz), sx, cc]
     s_kx, kx_came = Stream(kvb.at[0, pl.ds(0, NX - 1), 0]), new_sem()
-    for i in range(1, NX):
+    for i in farthest(NX):
         s_kx.send(own_kv, own_kv, cross_dev[i], kx_came)
     for step in (0, -1, 1):
         wx_first(lax.rem(sz + step + NZ, NZ))
@@ -326,15 +330,24 @@
     def cache_weight(origin):
         return kvb[pl.ds(4 * (origin // 4), 4), lax.rem(origin, NX)].reshape(WID, 2 * HD)
 
-    def reduce_send(step, way, chunk):
-        span = slice(chunk * ROWS, (chunk + 1) * ROWS)
-        slot = step * 2 + (0 if way == 1 else 1)
-        origin = lax.rem(hy + way * (NY // 2 - step) + NY, NY)
-        value = dot(hg[span, :], cache_weight(origin))
+    def toward(step, way):
+        return lax.rem(hy + way * (NY // 2 - step) + NY, NY)
+
+    def partial(origin, span):
+        return dot(hg[span, :], cache_weight(origin))
+
+    def side(way):
+        return 0 if way == 1 else 1
+
+    def rows_of(chunk):
+        return slice(chunk * ROWS, (chunk + 1) * ROWS)
+
+    def reduce_send(step, way, chunk, value):
+        slot = step * 2 + side(way)
         if (step - 1, way, chunk) in c_red:
             c_red[step - 1, way, chunk].wait_recv()
-            value = value + red_in[slot - 2, span, :].astype(F32)
-        red_out[slot, span, :] = value.astype(BF16)
+            value = value + red_in[slot - 2, rows_of(chunk), :].astype(F32)
+        red_out[slot, rows_of(chunk), :] = value.astype(BF16)
         c_red[step, way, chunk] = s_red.send(
             red_out.at[slot, pl.ds(chunk * ROWS, ROWS)], red_in.at[slot, pl.ds(chunk * ROWS, ROWS)],
             right_y if way == 1 else left_y, new_sem(),
@@ -342,35 +355,42 @@
 
     gain = gain_ref[...].astype(F32).reshape(1, WID)
     for chunk in ORDER:
-        span = slice(chunk * ROWS, (chunk + 1) * ROWS)
+        span = rows_of(chunk)
         c_mix[NY // 2, far(chunk), chunk].wait_recv()
         hidden = (acc[span, :] + dot(abuf[last, span, :], weight(last))).astype(BF16).astype(F32)
         hg[span, :] = (hidden * gain).astype(BF16)
         scol[span, :] = jnp.broadcast_to(jnp.sum(hidden * hidden, axis=1, keepdims=True), (ROWS, HD))
-        reduce_send(0, far(chunk), chunk)
-        reduce_send(1, -far(chunk), chunk)
+        for step, way in ((0, far(chunk)), (1, -far(chunk))):
+            reduce_send(step, way, chunk, partial(toward(step, way), span))
+    for way in (1, -1):
+        half = slice(0, TOK // 2) if way == 1 else slice(TOK // 2, TOK)
+        part[side(way), half, :] = partial(toward(1, way), half)
+    for chunk in ORDER:
+        way = far(chunk)
+        reduce_send(1, way, chunk, part[side(way), rows_of(chunk), :])
     sq[hy] = jnp.transpose(scol[...])[0:8, :]
     s_sq, sq_came = Stream(sq.at[pl.ds(0, NY - 1)]), new_sem()
-    for i in range(1, NY):
+    for i in farthest(NY):
         s_sq.send(sq.at[hy], sq.at[hy], head_dev[i], sq_came)
-    for chunk in ORDER:
-        reduce_send(1, far(chunk), chunk)
     for step in range(2, NY // 2):
+        for way in (1, -1):
+            part[side(way)] = partial(toward(step, way), slice(None))
         for late in (False, True):
             for chunk in ORDER:
-                reduce_send(step, far(chunk) if late else -far(chunk), chunk)
+                way = far(chunk) if late else -far(chunk)
+                reduce_send(step, way, chunk, part[side(way), rows_of(chunk), :])
+    part[0] = partial(hy, slice(None))
     arrived(sq.at[pl.ds(0, NY - 1)], sq_came)
     total = sq[0]
     for y in range(1, NY):
         total = total + sq[y]
     inverse = jnp.transpose(lax.rsqrt(total / (WID * NY) + 1e-6))
     for chunk in ORDER:
-        span = slice(chunk * ROWS, (chunk + 1) * ROWS)
-        value = dot(hg[span, :], cache_weight(hy))
+        span = rows_of(chunk)
+        value = part[0, span, :]
         for way in (1, -1):
             c_red[NY // 2 - 1, way, chunk].wait_recv()
-            slot = NY - 2 + (0 if way == 1 else 1)
-            value = value + red_in[slot, span, :].astype(F32)
+            value = value + red_in[NY - 2 + side(way), span, :].astype(F32)
         out_ref[span, :] = (value * inverse[span, 0:1]).astype(BF16)
 
     assert count[0] <= COPIES, count[0]
@@ -410,6 +430,7 @@
             pltpu.VMEM((TOK, WID), F32),
             block,
             reds, reds,
+            pltpu.VMEM((2, TOK, 2 * HD), F32),
             pltpu.VMEM((TOK, HD), F32),
             pltpu.VMEM((NY, 8, TOK), F32),
             pltpu.SemaphoreType.DMA((7,)),

time: 78.2 us -> 76.9 us (0.983); the launches traced: 76.6 us -> 76.5 us
  no operation moved by 1% of the time
where the time goes in v5:
time: 76.9 us; the launch traced here: 76.5 us
  Pallas kernels  74.3 us (97%)
  local copies, waits for them, and re-layouts  1.53 us (2%)
    pallas_call x1, Pallas kernels, on_device(): pl.pallas_call(layer_kernel, out_shape=jax.ShapeDtypeStruct((TOK, 2 * HD)...  74.3 us

profile of v5, /device:TPU:1, one launch (start us, length us, event | category | flops | bytes accessed | tf_op | source)
XLA Modules:
  0.0 76.5 jit_solution(9580289300559848438)
XLA Ops:
  0.6 74.3 %shard_map.104 = bf16[256,256]{1,0:T(8,128)(2,1)} custom-call(bf16[256,512]{1,0:T(8,128)(2,1)} %q_h.1, bf16[256,512]{1,0:T(8,128)(2,1)} %k_h.1, bf16[256,512]{1,0:T(8,128)(2,1)} %v_h.1, bf16[256,512]{1,0:T(8,128)(2,1)} %g_h.1, bf16[256,512]{1,0:T(8,128)(2,1)} %r_h.1, f32[4,256]{1,0:T(4,128)} %bitcast.1, bf16[64,512]{1,0:T(8,128)(2,1)} %ow_h.1, ...), custom_call_target="tpu_custom_call" | custom-call | tf_op jit(solution)/shard_map/pallas_call | solution.py:410
  75.0 1.5 %fusion = (bf16[256,128]{1,0:T(8,128)(2,1)}, bf16[256,128]{1,0:T(8,128)(2,1)}) fusion(bf16[256,256]{1,0:T(8,128)(2,1)} %shard_map.104), kind=kLoop, calls=%fused_computation | loop fusion | bytes 262144 | tf_op jit(solution)/shard_map/slice | solution.py:445

commit v6 on v5

--- a/solution.py
+++ b/solution.py
@@ -76,14 +76,6 @@
             device_id=home, device_id_type=MESH,
         ).wait_recv()
 
-    loads = {}
-    for i, (name, src, dst) in enumerate((
-        ("w", ow_h, wbuf.at[sx, sz, sc]), ("kw", kw_h, kin), ("k", k_h, k), ("v", v_h, v),
-        ("q", q_h, q), ("g", g_h, g), ("r", r_h, res),
-    )):
-        loads[name] = pltpu.make_async_copy(src, dst, lsem.at[i])
-        loads[name].start()
-
     swap_x, swap_z = lax.rem(hy, NX), jnp.where(hy < NX, sz, NZ - 1 - sz)
     swap_to = at(swap_x, swap_z, cc, 2 * sx + sz // 4)
 
@@ -101,6 +93,14 @@
     for device in greeted:
         pl.semaphore_signal(barrier, inc=1, device_id=device, device_id_type=MESH)
 
+    loads = {}
+    for i, (name, src, dst) in enumerate((
+        ("w", ow_h, wbuf.at[sx, sz, sc]), ("kw", kw_h, kin), ("k", k_h, k), ("v", v_h, v),
+        ("q", q_h, q), ("g", g_h, g), ("r", r_h, res),
+    )):
+        loads[name] = pltpu.make_async_copy(src, dst, lsem.at[i])
+        loads[name].start()
+
     rows = lax.broadcasted_iota(jnp.int32, (TOK, TOK), 0)
     cols = lax.broadcasted_iota(jnp.int32, (TOK, TOK), 1)
     lower = rows >= cols
@@ -195,11 +195,10 @@
     arrived(rs.at[pl.ds(0, GROUP - 1)], st_came)
     state = jnp.zeros((SLICE, HD), F32)
     passed = jnp.zeros((1, HD), F32)
-    before = []
     for i in range(GROUP):
         ex[i] = state
-        before.append(passed)
         step = dec[i]
+        dec[i] = passed
         state = jnp.exp(step) * state + rs[i].astype(F32)
         passed = passed + step
     xs[sx, 0:SLICE, :] = state
@@ -215,12 +214,12 @@
     for x in range(NX - 1):
         fresh = jnp.exp(xs[x, SLICE:SLICE + 1, :]) * base + xs[x, 0:SLICE, :]
         base = jnp.where(x < sx, fresh, base)
-    for i in range(GROUP):
-        ob[i] = (ex[i] + jnp.exp(before[i]) * base).astype(BF16)
     s_inc, inc_came = Stream(ob.at[pl.ds(0, GROUP - 1)]), new_sem()
     for i in farthest(GROUP):
-        s_inc.send(ob.at[group[i]], inc.at[p], group_dev[i], inc_came)
-    inc[p] = ob[p]
+        there = group[i]
+        ob[there] = (ex[there] + jnp.exp(dec[there]) * base).astype(BF16)
+        s_inc.send(ob.at[there], inc.at[p], group_dev[i], inc_came)
+    inc[p] = (ex[p] + jnp.exp(dec[p]) * base).astype(BF16)
 
     c_swap.wait_recv()
     own_kv = kvb.at[kslot(sz), sx, cc]

time: 76.9 us -> 76.9 us (level)
  no operation moved by 1% of the time
where the time goes in v6:
time: 76.9 us; the launch traced here: 76 us
  Pallas kernels  73.8 us (96%)
  local copies, waits for them, and re-layouts  1.53 us (2%)
    pallas_call x1, Pallas kernels, on_device(): pl.pallas_call(layer_kernel, out_shape=jax.ShapeDtypeStruct((TOK, 2 * HD)...  73.8 us

profile of v6, /device:TPU:1, one launch (start us, length us, event | category | flops | bytes accessed | tf_op | source)
XLA Modules:
  0.0 76.0 jit_solution(8691645576782935242)
XLA Ops:
  0.6 73.8 %shard_map.104 = bf16[256,256]{1,0:T(8,128)(2,1)} custom-call(bf16[256,512]{1,0:T(8,128)(2,1)} %q_h.1, bf16[256,512]{1,0:T(8,128)(2,1)} %k_h.1, bf16[256,512]{1,0:T(8,128)(2,1)} %v_h.1, bf16[256,512]{1,0:T(8,128)(2,1)} %g_h.1, bf16[256,512]{1,0:T(8,128)(2,1)} %r_h.1, f32[4,256]{1,0:T(4,128)} %bitcast.1, bf16[64,512]{1,0:T(8,128)(2,1)} %ow_h.1, ...), custom_call_target="tpu_custom_call" | custom-call | tf_op jit(solution)/shard_map/pallas_call | solution.py:409
  74.4 1.5 %fusion = (bf16[256,128]{1,0:T(8,128)(2,1)}, bf16[256,128]{1,0:T(8,128)(2,1)}) fusion(bf16[256,256]{1,0:T(8,128)(2,1)} %shard_map.104), kind=kLoop, calls=%fused_computation | loop fusion | bytes 262144 | tf_op jit(solution)/shard_map/slice | solution.py:444
